TPU v7x, 32 devices: a whole 2x2x4 slice. The times are simulated.
32 devices in a mesh: row: 4 (over y, x), col: 8 (over z, core).
Axes of the slice: x: 2, y: 2, z: 4, core: 2. Of those that a mesh axis runs over, the one named last changes fastest.
Arguments:
- points: bfloat16 [8192, 256], P(('row', 'col')), may hold values from -0.4 to 0.4, as said below
- spread: float32 [8192], P(('row', 'col')), may hold values from 1 to 12
- vectors: bfloat16 [8192, 64], P(('row', 'col')), may hold values from -6 to 6
Outputs:
- product: float32 [8192, 64], P(('row', 'col'))
Inputs may be any that keep to these rules, and one draw needn't show every extreme that they name: `points`: embedding entries are real values of order 0.1.
All inputs are finite; a program needn't handle non-finite values.
Results may differ from a plain program's by a relative error of at most 0.0085.
Values may be sent and summed in bfloat16 or wider, within the bound.
A program may use at most 128 MiB of HBM per device.

v0:
```python
import jax
import jax.numpy as jnp
from jax import lax
from jax.sharding import PartitionSpec as P


def distances(left_pts, right_pts):
    left_f = left_pts.astype(jnp.float32)
    right_f = right_pts.astype(jnp.float32)
    left_sq = jnp.sum(left_f * left_f, axis=1)
    right_sq = jnp.sum(right_f * right_f, axis=1)
    cross = lax.dot_general(
        left_pts, right_pts, (((1,), (1,)), ((), ())), preferred_element_type=jnp.float32
    )
    return left_sq[:, None] + right_sq[None, :] - 2.0 * cross


def local(points, spread, vectors):
    share_rows = points.shape[0]
    n_rows = lax.axis_size("row")
    n_cols = lax.axis_size("col")
    row_pos = lax.axis_index("row")
    col_pos = lax.axis_index("col")
    blk_pts, blk_bw, blk_vec = (
        lax.all_gather(points, "col", axis=0, tiled=True),
        lax.all_gather(spread.astype(jnp.bfloat16), "col", axis=0, tiled=True).astype(spread.dtype),
        lax.all_gather(vectors, "col", axis=0, tiled=True),
    )
    crs_pts, crs_bw, crs_vec = (
        lax.all_gather(points, "row", axis=0, tiled=True),
        lax.all_gather(spread.astype(jnp.bfloat16), "row", axis=0, tiled=True).astype(spread.dtype),
        lax.all_gather(vectors, "row", axis=0, tiled=True),
    )
    blk_local = jnp.arange(share_rows * n_cols, dtype=jnp.int32)
    blk_ids = row_pos * (n_cols * share_rows) + blk_local
    crs_local = jnp.arange(share_rows * n_rows, dtype=jnp.int32)
    crs_ids = (
        crs_local // share_rows * (n_cols * share_rows)
        + col_pos * share_rows
        + crs_local % share_rows
    )
    same = blk_ids[:, None] == crs_ids[None, :]
    dist = distances(blk_pts, crs_pts)
    kernel = jnp.where(same, jnp.float32(0.0), jnp.exp(-blk_bw[:, None] * dist))
    totals = lax.psum(jnp.sum(kernel, axis=1), "col")
    norm = (kernel / totals[:, None]).astype(jnp.bfloat16)
    to_cross = lax.dot_general(
        norm, blk_vec, (((0,), (0,)), ((), ())), preferred_element_type=jnp.float32
    )
    mirror = jnp.where(same, jnp.float32(0.0), jnp.exp(-crs_bw[None, :] * dist))
    mirror_tot = lax.psum(jnp.sum(mirror, axis=0), "row")
    mirror_norm = (mirror / mirror_tot[None, :]).astype(jnp.bfloat16)
    to_cross = to_cross + lax.dot_general(
        mirror_norm, blk_vec, (((0,), (0,)), ((), ())), preferred_element_type=jnp.float32
    )
    summed = lax.psum_scatter(to_cross, "row", scatter_dimension=0, tiled=True)
    return 0.5 * summed


def solution(mesh):
    placed = (P(("row", "col"), None), P(("row", "col")), P(("row", "col"), None))
    return jax.shard_map(
        local, mesh=mesh, in_specs=placed, out_specs=P(("row", "col"), None), check_vma=False
    )
```

profile of v0, /device:TPU:0, one launch (start us, length us, event | category | flops | bytes accessed | tf_op | source)
XLA Modules:
  0.0 126.9 jit_solution(6512187139585747209)
XLA Ops:
  6.5 0.0 all-gather.4.cloned.1.call-start
  6.5 0.7 all-gather.4.cloned.1.call-update
  7.3 0.0 reduce-scatter.2.cloned.1.call-start
  7.3 0.7 convert_element_type.22
  8.0 9.5 %all-gather.1 = bf16[4,1,256]{2,1,0:T(2,128)(2,1)S(1)} all-gather(bf16[1,1,256]{2,1,0:T(2,128)(2,1)S(1)} %reshape.35), channel_id=1, replica_groups=mesh['row'=4,'col'=8] {'row'}, dimensions={0}, use_global_device_ids=true | all-gather | bytes 2560 | tf_op jit(solution)/shard_map/all_gather | solution.py:31
  17.5 12.0 %all-gather = bf16[8,1,256]{2,1,0:T(2,128)(2,1)S(1)} all-gather(bf16[1,1,256]{2,1,0:T(2,128)(2,1)S(1)} %reshape.35), channel_id=1, replica_groups=mesh['row'=4,'col'=8] {'col'}, dimensions={0}, use_global_device_ids=true | all-gather | bytes 4608 | tf_op jit(solution)/shard_map/all_gather | solution.py:26
  29.5 10.3 %all_gather.17 = bf16[1024,256]{1,0:T(8,128)(2,1)S(1)} all-gather(bf16[256,256]{1,0:T(8,128)(2,1)} %param.3), channel_id=1, replica_groups=mesh['row'=4,'col'=8] {'row'}, dimensions={0}, use_global_device_ids=true | all-gather | bytes 655360 | tf_op jit(solution)/shard_map/all_gather | solution.py:30
  39.8 14.4 %all_gather.18 = bf16[2048,64]{0,1:T(8,128)(2,1)S(1)} all-gather(bf16[256,64]{0,1:T(8,128)(2,1)} %param.5), channel_id=1, replica_groups=mesh['row'=4,'col'=8] {'col'}, dimensions={0}, use_global_device_ids=true | all-gather | bytes 294912 | tf_op jit(solution)/shard_map/all_gather | solution.py:27
  54.2 0.2 multiply_reduce_fusion.1
  54.5 0.0 all-gather.4.cloned.1.call-done
  54.5 1.6 %multiply_reduce_fusion = f32[2048]{0:T(1024)S(1)} fusion(bf16[2048,256]{1,0:T(8,128)(2,1)} %all-gather.4.cloned.1.call-done), kind=kLoop, calls=%fused_computation.9 | loop fusion | flops 1570816 | bytes 1056768 | tf_op jit(solution)/shard_map/reduce_sum | solution.py:10
  56.1 7.5 %fusion = (f32[2048]{0:T(1024)S(1)}, f32[1024]{0:T(1024)S(1)}, f32[2048,1024]{1,0:T(8,128)}) fusion(f32[1024]{0:T(1024)S(1)} %multiply_reduce_fusion.1, f32[2048]{0:T(1024)S(1)} %multiply_reduce_fusion, f32[2048]{0:T(1024)S(1)} %bitcast.6, s32[1024]{0:T(1024)S(1)} %fusion.13, s32[2048]{0:T(1024)S(1)} %iota_add_fusion, f32[1024]{0:T(1024)S(1)} %bitcast.8, ...), kind=kOutput, calls=%fused_computation.5 | convolution fusion | flops 1094710272 | bytes 10010624 | tf_op jit(solution)/shard_map/dot_general | solution.py:12
  63.6 8.9 %psum.15 = f32[1024]{0:T(1024)S(1)} all-reduce(f32[1024]{0:T(1024)S(1)} %get-tuple-element.6), channel_id=1, replica_groups=mesh['row'=4,'col'=8] {'row'}, use_global_device_ids=true, to_apply=%region_5.6 | all-reduce | flops 1024 | bytes 8192 | tf_op jit(solution)/shard_map/psum | solution.py:51
  72.5 13.9 %psum.14 = f32[2048]{0:T(1024)S(1)} all-reduce(f32[2048]{0:T(1024)S(1)} %get-tuple-element.5), channel_id=1, replica_groups=mesh['row'=4,'col'=8] {'col'}, use_global_device_ids=true, to_apply=%region_3.4 | all-reduce | flops 2048 | bytes 16384 | tf_op jit(solution)/shard_map/psum | solution.py:45
  86.4 0.0 copy-start
  86.4 6.9 %fusion.2 = f32[1024,64]{0,1:T(8,128)S(1)} fusion(bf16[2048,64]{0,1:T(8,128)(2,1)S(1)} %all_gather.18, f32[2048,1024]{1,0:T(8,128)} %get-tuple-element.7, f32[1024]{0:T(1024)S(1)} %psum.15, f32[1024]{0:T(1024)S(1)} %bitcast.9, f32[1024]{0:T(1024)S(1)} %multiply_reduce_fusion.1, f32[2048]{0:T(1024)S(1)} %multiply_reduce_fusion, s32[1024]{0:T(1024)S(1)} %fusion.13, ...), kind=kOutput, calls=%fused_computation.7 | convolution fusion | flops 285212672 | bytes 8945664 | tf_op jit(solution)/shard_map/dot_general | solution.py:53
  93.3 0.0 copy-done
  93.3 3.8 %fusion.4 = f32[1024,64]{0,1:T(8,128)} fusion(f32[1024,64]{0,1:T(8,128)S(1)} %fusion.2, bf16[2048,64]{0,1:T(8,128)(2,1)S(1)} %all_gather.18, f32[2048,1024]{1,0:T(8,128)S(1)} %copy-done, f32[2048]{0:T(1024)S(1)} %psum.14, f32[1024]{0:T(1024)S(1)} %multiply_reduce_fusion.1, f32[2048]{0:T(1024)S(1)} %multiply_reduce_fusion, f32[2048]{0:T(1024)S(1)} %bitcast.7, ...), kind=kOutput, calls=%fused_computation.10 | convolution fusion | flops 285278208 | bytes 9216000 | tf_op jit(solution)/shard_map/dot_general | solution.py:47
  97.1 0.0 reduce-scatter.2.cloned.1.call-update
  97.2 21.5 %reduce-scatter.2.cloned.1.call-done = f32[256,64]{0,1:T(8,128)} async-done(((f32[1024,64]{0,1:T(8,128)}), f32[256,64]{0,1:T(8,128)}) %reduce-scatter.2.cloned.1.call-update) | async-done | bytes 65552 | tf_op jit(solution)/shard_map/reduce_scatter | solution.py:56
  118.6 1.5 %broadcast_multiply_fusion = f32[256,64]{0,1:T(8,128)} fusion(f32[256,64]{0,1:T(8,128)} %reduce-scatter.2.cloned.1.call-done), kind=kLoop, calls=%fused_computation.12 | loop fusion | flops 16384 | bytes 131072 | tf_op jit(solution)/shard_map/mul | solution.py:57
  (5 shorter events, 0.0 us)
Async XLA Ops:
  6.5 47.9 %all-gather.4.cloned.1.call-start = ((), (), s32[]{:S(2)}) async-start(), calls=%async_computation.1 | async-start | bytes 1179648 | tf_op jit(solution)/shard_map/all_gather | solution.py:25
  7.3 111.4 %reduce-scatter.2.cloned.1.call-start = ((), (), s32[]{:S(2)}) async-start(), calls=%async_computation.2 | async-start | bytes 327680 | tf_op jit(solution)/shard_map/reduce_scatter | solution.py:56
  86.4 6.9 %copy-start = (f32[2048,1024]{1,0:T(8,128)S(1)}, f32[2048,1024]{1,0:T(8,128)}, u32[]{:S(2)}) copy-start(f32[2048,1024]{1,0:T(8,128)} %get-tuple-element.7) | copy-start | bytes 25165828
Sparse Core Ops, SparseCore 0:
  9.0 24.7 all-gather.3
  97.3 21.3 reduce-scatter.1
where the time goes:
time: 127 us
  blocking collectives  69 us (54%)
  waiting for transfers between devices  22.2 us (17%)
  matrix products  18.2 us (14%)
  between operations  13.5 us (11%)
  other arithmetic  3.97 us (3%)
    reduce_scatter x1, waiting for transfers between devices, local(): summed = lax.psum_scatter(to_cross, 'row', scatter_dimension=0, tiled=True)  21.5 us
    all_gather x1, blocking collectives, local(): lax.all_gather(vectors, 'col', axis=0, tiled=True)  14.4 us
    psum x1, blocking collectives, local(): totals = lax.psum(jnp.sum(kernel, axis=1), 'col')  13.9 us
    all_gather x1, blocking collectives, local(): lax.all_gather(spread.astype(jnp.bfloat16), 'col', axis=0, tiled=True)  12 us
    all_gather x1, blocking collectives, local(): lax.all_gather(points, 'row', axis=0, tiled=True)  10.3 us
    all_gather x1, blocking collectives, local(): lax.all_gather(spread.astype(jnp.bfloat16), 'row', axis=0, tiled=True)  9.5 us
    psum x1, blocking collectives, local(): mirror_tot = lax.psum(jnp.sum(mirror, axis=0), 'row')  8.9 us
    dot_general x1, matrix products, distances(): lax.dot_general(left_pts, right_pts, (((1,), (1,)), ((), ())), preferred_...  7.5 us
  transfers between devices with their start and end apart: 2, of which 1 were waited for; matrix products, arithmetic and copies ran while one was open for 1% of the time, Pallas kernels for 0%

commit v1 on v0

--- a/solution.py
+++ b/solution.py
@@ -2,6 +2,18 @@
 import jax.numpy as jnp
 from jax import lax
 from jax.sharding import PartitionSpec as P
+
+
+def doubled_up(array, axis, dim):
+    ways, here = (lax.axis_size(axis), lax.axis_index(axis))
+    grown, reach = (array, 1)
+    while reach < ways:
+        theirs = lax.ppermute(grown, axis, [(d, d ^ reach) for d in range(ways)])
+        mine_first = jnp.concatenate([grown, theirs], axis=dim)
+        theirs_first = jnp.concatenate([theirs, grown], axis=dim)
+        grown = jnp.where(here & reach == 0, mine_first, theirs_first)
+        reach = 2 * reach
+    return grown
 
 
 def distances(left_pts, right_pts):
@@ -28,7 +40,7 @@
     )
     crs_pts, crs_bw, crs_vec = (
         lax.all_gather(points, "row", axis=0, tiled=True),
-        lax.all_gather(spread.astype(jnp.bfloat16), "row", axis=0, tiled=True).astype(spread.dtype),
+        doubled_up(spread.astype(jnp.bfloat16), "row", 0).astype(spread.dtype),
         lax.all_gather(vectors, "row", axis=0, tiled=True),
     )
     blk_local = jnp.arange(share_rows * n_cols, dtype=jnp.int32)

time: 127 us -> 124 us (0.976)
  blocking collectives: 69 us -> 59.6 us
  starting transfers between devices: 0.04 us -> 4.52 us
  waiting for transfers between devices: 22.2 us -> 24.3 us
    all_gather x1 -> x0, blocking collectives: 9.5 us -> none  [local(): lax.all_gather(spread.astype(jnp.bfloat16), 'row', axis=0, tiled=True)]
    ppermute x0 -> x2, starting transfers between devices: none -> 4.48 us  [doubled_up(): theirs = lax.ppermute(grown, axis, [(d, d ^ reach) for d in range(ways)])]
    ppermute x0 -> x2, waiting for transfers between devices: none -> 2.09 us  [doubled_up(): theirs = lax.ppermute(grown, axis, [(d, d ^ reach) for d in range(ways)])]
  transfers between devices with their start and end apart: 2 -> 4, of which waited for: 1 -> 2; matrix products, arithmetic and copies ran while one was open for 1% -> 1% of each run, Pallas kernels for 0% -> 0%
where the time goes in v1:
time: 124 us
  blocking collectives  59.6 us (48%)
  waiting for transfers between devices  24.3 us (20%)
  matrix products  18.2 us (15%)
  between operations  13.5 us (11%)
  starting transfers between devices  4.52 us (4%)
  other arithmetic  3.98 us (3%)
    reduce_scatter x1, waiting for transfers between devices, local(): summed = lax.psum_scatter(to_cross, 'row', scatter_dimension=0, tiled=True)  21.5 us
    all_gather x1, blocking collectives, local(): lax.all_gather(vectors, 'col', axis=0, tiled=True)  14.4 us
    psum x1, blocking collectives, local(): totals = lax.psum(jnp.sum(kernel, axis=1), 'col')  13.9 us
    all_gather x1, blocking collectives, local(): lax.all_gather(spread.astype(jnp.bfloat16), 'col', axis=0, tiled=True)  12 us
    all_gather x1, blocking collectives, local(): lax.all_gather(points, 'row', axis=0, tiled=True)  10.4 us
    psum x1, blocking collectives, local(): mirror_tot = lax.psum(jnp.sum(mirror, axis=0), 'row')  8.91 us
    dot_general x1, matrix products, distances(): lax.dot_general(left_pts, right_pts, (((1,), (1,)), ((), ())), preferred_...  7.47 us
    dot_general x1, matrix products, local(): lax.dot_general(mirror_norm, blk_vec, (((0,), (0,)), ((), ())), preferred...  6.88 us
  transfers between devices with their start and end apart: 4, of which 2 were waited for; matrix products, arithmetic and copies ran while one was open for 1% of the time, Pallas kernels for 0%

profile of v1, /device:TPU:0, one launch (start us, length us, event | category | flops | bytes accessed | tf_op | source)
XLA Modules:
  0.0 124.1 jit_solution(7497700386192561572)
XLA Ops:
  6.5 0.0 all-gather.3.cloned.1.call-start
  6.5 0.7 all-gather.3.cloned.1.call-update
  7.3 0.0 reduce-scatter.2.cloned.1.call-start
  7.3 0.7 convert_element_type.26
  8.0 2.9 %collective-permute-start = (bf16[256]{0:T(256)(128)(2,1)S(1)}, bf16[256]{0:T(256)(128)(2,1)S(1)}, u32[]{:S(2)}, u32[]{:S(2)}) collective-permute-start(bf16[256]{0:T(256)(128)(2,1)S(1)} %convert_element_type.26), channel_id=1, source_target_pairs={{0,8},{8,0},{16,24},{24,16},{1,9},{9,1},{17,25},{25,17},{2,10},{10... | collective-permute-start | bytes 1544 | tf_op jit(solution)/shard_map/ppermute | solution.py:11
  10.9 12.0 %all-gather = bf16[8,1,256]{2,1,0:T(2,128)(2,1)S(1)} all-gather(bf16[1,1,256]{2,1,0:T(2,128)(2,1)S(1)} %reshape.81), channel_id=1, replica_groups=mesh['row'=4,'col'=8] {'col'}, dimensions={0}, use_global_device_ids=true | all-gather | bytes 4608 | tf_op jit(solution)/shard_map/all_gather | solution.py:38
  22.9 10.4 %all_gather.14 = bf16[1024,256]{1,0:T(8,128)(2,1)S(1)} all-gather(bf16[256,256]{1,0:T(8,128)(2,1)} %param.3), channel_id=1, replica_groups=mesh['row'=4,'col'=8] {'row'}, dimensions={0}, use_global_device_ids=true | all-gather | bytes 655360 | tf_op jit(solution)/shard_map/all_gather | solution.py:42
  33.3 14.4 %all_gather.15 = bf16[2048,64]{0,1:T(8,128)(2,1)S(1)} all-gather(bf16[256,64]{0,1:T(8,128)(2,1)} %param.5), channel_id=1, replica_groups=mesh['row'=4,'col'=8] {'col'}, dimensions={0}, use_global_device_ids=true | all-gather | bytes 294912 | tf_op jit(solution)/shard_map/all_gather | solution.py:39
  47.7 0.2 multiply_reduce_fusion.1
  48.0 0.0 collective-permute-done
  48.0 1.5 %collective-permute-start.1 = (bf16[512]{0:T(512)(128)(2,1)S(1)}, bf16[512]{0:T(512)(128)(2,1)S(1)}, u32[]{:S(2)}, u32[]{:S(2)}) collective-permute-start(bf16[512]{0:T(512)(128)(2,1)S(1)} %maximum_select_fusion.1), channel_id=1, source_target_pairs={{0,16},{8,24},{16,0},{24,8},{1,17},{9,25},{17,1},{25,9},{2,18},{10... | collective-permute-start | bytes 3080 | tf_op jit(solution)/shard_map/ppermute | solution.py:11
  49.6 2.1 %collective-permute-done.1 = bf16[512]{0:T(512)(128)(2,1)S(1)} collective-permute-done((bf16[512]{0:T(512)(128)(2,1)S(1)}, bf16[512]{0:T(512)(128)(2,1)S(1)}, u32[]{:S(2)}, u32[]{:S(2)}) %collective-permute-start.1) | collective-permute-done | bytes 1056 | tf_op jit(solution)/shard_map/ppermute | solution.py:11
  51.7 0.0 all-gather.3.cloned.1.call-done
  51.7 1.6 %multiply_reduce_fusion = f32[2048]{0:T(1024)S(1)} fusion(bf16[2048,256]{1,0:T(8,128)(2,1)} %all-gather.3.cloned.1.call-done), kind=kLoop, calls=%fused_computation.9 | loop fusion | flops 1570816 | bytes 1056768 | tf_op jit(solution)/shard_map/reduce_sum | solution.py:22
  53.3 7.5 %fusion = (f32[2048]{0:T(1024)S(1)}, f32[1024]{0:T(1024)S(1)}, f32[2048,1024]{1,0:T(8,128)}) fusion(f32[1024]{0:T(1024)S(1)} %multiply_reduce_fusion.1, f32[2048]{0:T(1024)S(1)} %multiply_reduce_fusion, f32[2048]{0:T(1024)S(1)} %bitcast.5, s32[1024]{0:T(1024)S(1)} %fusion.13, s32[2048]{0:T(1024)S(1)} %iota_add_fusion, f32[1024]{0:T(1024)S(1)} %convert_negate_fusion.1, ...), kind=kOutput, calls=%fused_computation.5 | convolution fusion | flops 1094710272 | bytes 10010624 | tf_op jit(solution)/shard_map/dot_general | solution.py:24
  60.7 8.9 %psum.15 = f32[1024]{0:T(1024)S(1)} all-reduce(f32[1024]{0:T(1024)S(1)} %get-tuple-element.6), channel_id=1, replica_groups=mesh['row'=4,'col'=8] {'row'}, use_global_device_ids=true, to_apply=%region_5.6 | all-reduce | flops 1024 | bytes 8192 | tf_op jit(solution)/shard_map/psum | solution.py:63
  69.6 13.9 %psum.14 = f32[2048]{0:T(1024)S(1)} all-reduce(f32[2048]{0:T(1024)S(1)} %get-tuple-element.5), channel_id=1, replica_groups=mesh['row'=4,'col'=8] {'col'}, use_global_device_ids=true, to_apply=%region_3.4 | all-reduce | flops 2048 | bytes 16384 | tf_op jit(solution)/shard_map/psum | solution.py:57
  83.5 0.0 copy-start
  83.6 6.9 %fusion.2 = f32[1024,64]{0,1:T(8,128)S(1)} fusion(bf16[2048,64]{0,1:T(8,128)(2,1)S(1)} %all_gather.15, f32[2048,1024]{1,0:T(8,128)} %get-tuple-element.7, f32[1024]{0:T(1024)S(1)} %psum.15, f32[1024]{0:T(1024)S(1)} %convert_negate_fusion.1, f32[1024]{0:T(1024)S(1)} %multiply_reduce_fusion.1, f32[2048]{0:T(1024)S(1)} %multiply_reduce_fusion, ...), kind=kOutput, calls=%fused_computation.7 | convolution fusion | flops 285212672 | bytes 8945664 | tf_op jit(solution)/shard_map/dot_general | solution.py:65
  90.4 0.0 copy-done
  90.5 3.8 %fusion.4 = f32[1024,64]{0,1:T(8,128)} fusion(f32[1024,64]{0,1:T(8,128)S(1)} %fusion.2, bf16[2048,64]{0,1:T(8,128)(2,1)S(1)} %all_gather.15, f32[2048,1024]{1,0:T(8,128)S(1)} %copy-done, f32[2048]{0:T(1024)S(1)} %psum.14, f32[1024]{0:T(1024)S(1)} %multiply_reduce_fusion.1, f32[2048]{0:T(1024)S(1)} %multiply_reduce_fusion, f32[2048]{0:T(1024)S(1)} %bitcast.6, ...), kind=kOutput, calls=%fused_computation.10 | convolution fusion | flops 285278208 | bytes 9216000 | tf_op jit(solution)/shard_map/dot_general | solution.py:59
  94.3 0.0 reduce-scatter.2.cloned.1.call-update
  94.3 21.5 %reduce-scatter.2.cloned.1.call-done = f32[256,64]{0,1:T(8,128)} async-done(((f32[1024,64]{0,1:T(8,128)}), f32[256,64]{0,1:T(8,128)}) %reduce-scatter.2.cloned.1.call-update) | async-done | bytes 65552 | tf_op jit(solution)/shard_map/reduce_scatter | solution.py:68
  115.8 1.5 %broadcast_multiply_fusion = f32[256,64]{0,1:T(8,128)} fusion(f32[256,64]{0,1:T(8,128)} %reduce-scatter.2.cloned.1.call-done), kind=kLoop, calls=%fused_computation.12 | loop fusion | flops 16384 | bytes 131072 | tf_op jit(solution)/shard_map/mul | solution.py:69
  (6 shorter events, 0.0 us)
Async XLA Ops:
  6.5 45.1 %all-gather.3.cloned.1.call-start = ((), (), s32[]{:S(2)}) async-start(), calls=%async_computation.1 | async-start | bytes 1179648 | tf_op jit(solution)/shard_map/all_gather | solution.py:37
  7.3 108.5 %reduce-scatter.2.cloned.1.call-start = ((), (), s32[]{:S(2)}) async-start(), calls=%async_computation.2 | async-start | bytes 327680 | tf_op jit(solution)/shard_map/reduce_scatter | solution.py:68
  8.0 40.0 %collective-permute-start = (bf16[256]{0:T(256)(128)(2,1)S(1)}, bf16[256]{0:T(256)(128)(2,1)S(1)}, u32[]{:S(2)}, u32[]{:S(2)}) collective-permute-start(bf16[256]{0:T(256)(128)(2,1)S(1)} %convert_element_type.26), channel_id=1, source_target_pairs={{0,8},{8,0},{16,24},{24,16},{1,9},{9,1},{17,25},{25,17},{2,10},{10... | collective-permute-start | bytes 1544 | tf_op jit(solution)/shard_map/ppermute | solution.py:11
  48.0 3.6 %collective-permute-start.1 = (bf16[512]{0:T(512)(128)(2,1)S(1)}, bf16[512]{0:T(512)(128)(2,1)S(1)}, u32[]{:S(2)}, u32[]{:S(2)}) collective-permute-start(bf16[512]{0:T(512)(128)(2,1)S(1)} %maximum_select_fusion.1), channel_id=1, source_target_pairs={{0,16},{8,24},{16,0},{24,8},{1,17},{9,25},{17,1},{25,9},{2,18},{10... | collective-permute-start | bytes 3080 | tf_op jit(solution)/shard_map/ppermute | solution.py:11
  83.5 6.9 %copy-start = (f32[2048,1024]{1,0:T(8,128)S(1)}, f32[2048,1024]{1,0:T(8,128)}, u32[]{:S(2)}) copy-start(f32[2048,1024]{1,0:T(8,128)} %get-tuple-element.7) | copy-start | bytes 25165828
Sparse Core Ops, SparseCore 0:
  9.0 24.8 all-gather.2
  94.4 21.3 reduce-scatter.1
